TPU v7x, 32 devices: a whole 2x2x4 slice. The times are simulated.
32 devices in a mesh: dp: 16 (over z, y, core), mp: 2 (over x).
Axes of the slice: x: 2, y: 2, z: 4, core: 2. Of those that a mesh axis runs over, the one named last changes fastest.
Arguments:
- tokens: bfloat16 [4096, 2048], P(('dp', 'mp')), may hold values from -6 to 6
- doc_lengths: int32 [16, 6], P('dp'), may hold values from 1 to 128, 256 in all within a row
- cotangent: bfloat16 [4096, 2048], P(('dp', 'mp')), may hold values from -6 to 6
- gain_attn: float32 [2048], replicated, may hold values from 0.1 to 1.9
- gain_mlp: float32 [2048], replicated, may hold values from 0.1 to 1.9
- w_qkv: float32 [2048, 3, 2048], P('dp', None, 'mp'), may hold values from -0.1875 to 0.1875
- w_out: float32 [2048, 2048], P('mp', 'dp'), may hold values from -0.375 to 0.375
- w_gate_up: float32 [2048, 2, 5632], P('dp', None, 'mp'), may hold values from -0.125 to 0.125
- w_down: float32 [5632, 2048], P('mp', 'dp'), may hold values from -0.078125 to 0.078125
Outputs:
- block_out: bfloat16 [4096, 2048], P(('dp', 'mp'))
- input_grad: float32 [4096, 2048], P(('dp', 'mp'))
- grad_w_qkv: float32 [2048, 3, 2048], P('dp', None, 'mp')
- grad_w_out: float32 [2048, 2048], P('mp', 'dp')
- grad_w_gate_up: float32 [2048, 2, 5632], P('dp', None, 'mp')
- grad_w_down: float32 [5632, 2048], P('mp', 'dp')
- grad_gain_attn: float32 [2048], replicated
- grad_gain_mlp: float32 [2048], replicated
Inputs may be any that keep to these rules, and one draw needn't show every extreme that they name: `doc_lengths`: each packed row's 6 lengths sum to 256, and the longest of each row is exactly 128.
All inputs are finite; a program needn't handle non-finite values.
Results may differ from a plain program's by a relative error of at most 0.014.
The roundings to bfloat16 on the way count: a program that leaves them out, or rounds other values in their place, can miss the bound.
Values may be sent and summed in bfloat16 or wider, within the bound.
No kernel may reach another device: no remote copies, remote signals or barrier semaphores. Data moves between devices by JAX's collectives and lax.ppermute only.
A program may use at most 256 MiB of HBM per device.

v0:
```python
import jax
import jax.numpy as jnp
from jax import lax
from jax.sharding import PartitionSpec as P

HD = 128


EPSILON = 1e-05
MASKED = -1e30


def row_layout(lengths, row_len):
    doc_ends = jnp.cumsum(lengths)
    places = jnp.arange(row_len, dtype=jnp.int32)
    segment = jnp.sum((places[:, None] >= doc_ends[None, :]).astype(jnp.int32), axis=1)
    starts = doc_ends - lengths
    chosen = segment[:, None] == jnp.arange(lengths.shape[0], dtype=jnp.int32)[None, :]
    doc_start = jnp.sum(jnp.where(chosen, starts[None, :], 0), axis=1)
    return (segment, places - doc_start, places)


def rotary_tables(offsets, head_size):
    half_size = head_size // 2
    frequency = 10000.0 ** (-2.0 * jnp.arange(half_size, dtype=jnp.float32) / head_size)
    angles = offsets.astype(jnp.float32)[:, None] * frequency[None, :]
    return (jnp.cos(angles), jnp.sin(angles))


def rotate(field, cosine, sine_table):
    half_size = field.shape[-1] // 2
    front_half = field[..., :half_size]
    back_half = field[..., half_size:]
    cos_rows = cosine[:, None, :]
    sin_rows = sine_table[:, None, :]
    return jnp.concatenate(
        [
            front_half * cos_rows - back_half * sin_rows,
            back_half * cos_rows + front_half * sin_rows,
        ],
        axis=-1,
    )


def rotate_back(gradient, cosine, sine_table):
    half_size = gradient.shape[-1] // 2
    front_half = gradient[..., :half_size]
    back_half = gradient[..., half_size:]
    cos_rows = cosine[:, None, :]
    sin_rows = sine_table[:, None, :]
    return jnp.concatenate(
        [
            front_half * cos_rows + back_half * sin_rows,
            back_half * cos_rows - front_half * sin_rows,
        ],
        axis=-1,
    )


def norm_scale(field):
    return lax.rsqrt(jnp.mean(field * field, axis=-1, keepdims=True) + EPSILON)


def norm_back(grad_normed, field, gain_vec):
    inverse = norm_scale(field)
    normed = field * inverse
    scaled = grad_normed * gain_vec
    grad_field = inverse * (scaled - normed * jnp.mean(scaled * normed, axis=-1, keepdims=True))
    return (grad_field, jnp.sum(grad_normed * normed, axis=0))


def masked_scores(query_block, keys_rot, seg_rows, segment, place_rows, places, scale):
    raw_scores = jnp.einsum(
        "qhe,khe->hqk", query_block, keys_rot, preferred_element_type=jnp.float32
    )
    allowed = (seg_rows[:, None] == segment[None, :]) & (places[None, :] <= place_rows[:, None])
    return jnp.where(allowed[None], raw_scores * scale, MASKED)


def on_device(tokens, doc_lengths, cotangent, gain_attn, gain_mlp, w_qkv, w_out, w_gate_up, w_down):
    local_rows = tokens.shape[0]
    row_len = local_rows * lax.axis_size("mp")
    segment, offsets, places = row_layout(doc_lengths[0], row_len)
    cosine, sine_table = rotary_tables(offsets, HD)
    scale = HD ** (-0.5)
    block_count = max(1, row_len // 512)
    block_len = row_len // block_count
    block_starts = jnp.arange(block_count, dtype=jnp.int32) * block_len
    masters = (
        w_qkv.astype(jnp.bfloat16),
        w_out.astype(jnp.bfloat16),
        w_gate_up.astype(jnp.bfloat16),
        w_down.astype(jnp.bfloat16),
    )
    w_qkv_all, w_out_all, w_gu_all, w_down_all = (
        lax.all_gather(masters[0], "dp", axis=0, tiled=True),
        lax.all_gather(masters[1], "dp", axis=1, tiled=True),
        lax.all_gather(masters[2], "dp", axis=0, tiled=True),
        lax.all_gather(masters[3], "dp", axis=1, tiled=True),
    )
    resid_in = tokens.astype(jnp.float32)
    normed_attn = (resid_in * norm_scale(resid_in) * gain_attn).astype(jnp.bfloat16)
    attn_rows = lax.all_gather(normed_attn, "mp", axis=0, tiled=True)
    projected = jnp.einsum("td,dce->cte", attn_rows, w_qkv_all, preferred_element_type=jnp.float32)
    local_dim = projected.shape[2]
    local_heads = local_dim // HD
    projected = projected.reshape(3, row_len, local_heads, HD)
    queries = rotate(projected[0], cosine, sine_table).astype(jnp.bfloat16)
    keys_rot = rotate(projected[1], cosine, sine_table).astype(jnp.bfloat16)
    values_low = projected[2].astype(jnp.bfloat16)

    def forward_block(row_start):
        scores = masked_scores(queries, keys_rot, segment, segment, places, places, scale)
        row_max = jnp.max(scores, axis=-1, keepdims=True)
        exp_scores = jnp.exp(scores - row_max)
        denominator = jnp.sum(exp_scores, axis=-1, keepdims=True)
        attn_probs = (exp_scores / denominator).astype(jnp.bfloat16)
        mixed = jnp.einsum(
            "hqk,khe->qhe", attn_probs, values_low, preferred_element_type=jnp.float32
        )
        return (mixed.astype(jnp.bfloat16), (row_max + jnp.log(denominator))[..., 0])

    mixed_blocks, log_total = lax.map(forward_block, block_starts)
    mixed_rows = mixed_blocks.reshape(row_len, local_dim)
    part_rows = mixed_rows
    attn_part = lax.psum_scatter(
        jnp.dot(part_rows, w_out_all, preferred_element_type=jnp.float32),
        "mp",
        scatter_dimension=0,
        tiled=True,
    )
    resid_mid = resid_in + attn_part
    normed_mlp = (resid_mid * norm_scale(resid_mid) * gain_mlp).astype(jnp.bfloat16)
    mlp_rows = lax.all_gather(normed_mlp, "mp", axis=0, tiled=True)
    gate_up = jnp.einsum("td,dcf->ctf", mlp_rows, w_gu_all, preferred_element_type=jnp.float32)
    gate_sig = jax.nn.sigmoid(gate_up[0])
    gate_act = gate_up[0] * gate_sig
    hidden = (gate_act * gate_up[1]).astype(jnp.bfloat16)
    part_rows = hidden
    mlp_part = lax.psum_scatter(
        jnp.dot(part_rows, w_down_all, preferred_element_type=jnp.float32).astype(jnp.bfloat16),
        "mp",
        scatter_dimension=0,
        tiled=True,
    ).astype(jnp.float32)
    block_out = (resid_mid + mlp_part).astype(jnp.bfloat16)
    w_qkv_all, w_out_all, w_gu_all, w_down_all = (
        lax.all_gather(masters[0], "dp", axis=0, tiled=True),
        lax.all_gather(masters[1], "dp", axis=1, tiled=True),
        lax.all_gather(masters[2], "dp", axis=0, tiled=True),
        lax.all_gather(masters[3], "dp", axis=1, tiled=True),
    )
    grad_rows = lax.all_gather(cotangent, "mp", axis=0, tiled=True)
    grad_down = jnp.einsum("tf,td->fd", hidden, grad_rows, preferred_element_type=jnp.float32)
    d_hidden = jnp.einsum("td,fd->tf", grad_rows, w_down_all, preferred_element_type=jnp.float32)
    d_gate = d_hidden * gate_up[1] * gate_sig * (1.0 + gate_up[0] * (1.0 - gate_sig))
    d_up = d_hidden * gate_act
    d_gate_up = jnp.stack([d_gate, d_up]).astype(jnp.bfloat16)
    grad_gate_up = jnp.einsum(
        "td,ctf->dcf", mlp_rows, d_gate_up, preferred_element_type=jnp.float32
    )
    mlp_sums = (grad_gate_up, grad_down)
    part_rows = d_gate_up
    d_normed_mlp = lax.psum_scatter(
        jnp.einsum("ctf,dcf->td", part_rows, w_gu_all, preferred_element_type=jnp.float32),
        "mp",
        scatter_dimension=0,
        tiled=True,
    )
    d_resid_norm, gain_mlp_part = norm_back(d_normed_mlp, resid_mid, gain_mlp)
    d_resid_mid = d_resid_norm + cotangent.astype(jnp.float32)
    attn_grad_rows = lax.all_gather(d_resid_mid.astype(jnp.bfloat16), "mp", axis=0, tiled=True)
    grad_out = jnp.einsum(
        "te,td->ed", mixed_rows, attn_grad_rows, preferred_element_type=jnp.float32
    )
    d_mixed = jnp.einsum("td,ed->te", attn_grad_rows, w_out_all, preferred_element_type=jnp.float32)
    d_mixed = d_mixed.astype(jnp.bfloat16).reshape(row_len, local_heads, HD)

    def backward_block(running, pieces):
        d_keys_sum, d_values_sum = running
        row_start, log_block = pieces
        scores = masked_scores(queries, keys_rot, segment, segment, places, places, scale)
        attn_probs = jnp.exp(scores - log_block[..., None])
        d_probs = jnp.einsum(
            "qhe,khe->hqk", d_mixed, values_low, preferred_element_type=jnp.float32
        )
        row_dot = jnp.sum(attn_probs * d_probs, axis=-1, keepdims=True)
        d_raw = (attn_probs * (d_probs - row_dot) * scale).astype(jnp.bfloat16)
        d_query_block = jnp.einsum(
            "hqk,khe->qhe", d_raw, keys_rot, preferred_element_type=jnp.float32
        )
        d_keys_sum = d_keys_sum + jnp.einsum(
            "hqk,qhe->khe", d_raw, queries, preferred_element_type=jnp.float32
        )
        d_values_sum = d_values_sum + jnp.einsum(
            "hqk,qhe->khe",
            attn_probs.astype(jnp.bfloat16),
            d_mixed,
            preferred_element_type=jnp.float32,
        )
        return ((d_keys_sum, d_values_sum), d_query_block)

    zero_heads = jnp.zeros((row_len, local_heads, HD), jnp.float32)
    (d_keys, d_values), d_query_blocks = lax.scan(
        backward_block, (zero_heads, zero_heads), (block_starts, log_total)
    )
    d_queries = d_query_blocks.reshape(row_len, local_heads, HD)
    d_projected = jnp.stack(
        [
            rotate_back(d_queries, cosine, sine_table),
            rotate_back(d_keys, cosine, sine_table),
            d_values,
        ]
    )
    d_projected = d_projected.astype(jnp.bfloat16).reshape(3, row_len, local_dim)
    grad_qkv = jnp.einsum("td,cte->dce", attn_rows, d_projected, preferred_element_type=jnp.float32)
    part_rows = d_projected
    d_normed_attn = lax.psum_scatter(
        jnp.einsum("cte,dce->td", part_rows, w_qkv_all, preferred_element_type=jnp.float32).astype(
            jnp.bfloat16
        ),
        "mp",
        scatter_dimension=0,
        tiled=True,
    ).astype(jnp.float32)
    d_resid_first, gain_attn_part = norm_back(d_normed_attn, resid_in, gain_attn)
    input_grad = d_resid_mid + d_resid_first
    gain_totals = lax.psum((gain_attn_part, gain_mlp_part), ("dp", "mp"))
    weight_sums = (
        lax.psum_scatter(grad_qkv, "dp", scatter_dimension=0, tiled=True),
        lax.psum_scatter(grad_out, "dp", scatter_dimension=1, tiled=True),
        lax.psum_scatter(mlp_sums[0], "dp", scatter_dimension=0, tiled=True),
        lax.psum_scatter(mlp_sums[1], "dp", scatter_dimension=1, tiled=True),
    )
    return (
        block_out,
        input_grad,
        weight_sums[0],
        weight_sums[1],
        weight_sums[2],
        weight_sums[3],
        gain_totals[0],
        gain_totals[1],
    )


def solution(mesh):
    return jax.shard_map(
        on_device,
        mesh=mesh,
        in_specs=(
            P(("dp", "mp"), None),
            P("dp", None),
            P(("dp", "mp"), None),
            P(),
            P(),
            P("dp", None, "mp"),
            P("mp", "dp"),
            P("dp", None, "mp"),
            P("mp", "dp"),
        ),
        out_specs=(
            P(("dp", "mp"), None),
            P(("dp", "mp"), None),
            P("dp", None, "mp"),
            P("mp", "dp"),
            P("dp", None, "mp"),
            P("mp", "dp"),
            P(),
            P(),
        ),
        check_vma=False,
    )
```

profile of v0, /device:TPU:0, one launch (start us, length us, event | category | flops | bytes accessed | tf_op | source)
XLA Modules:
  0.0 1687.3 jit_solution(7793531926723083009)
XLA Ops:
  7.2 1.3 fusion.34
  8.6 0.5 copy-done.28
  9.1 2.0 fusion.31
  11.2 1.0 convert_element_type.88
  12.3 0.7 convert_element_type.95
  13.6 0.5 multiply_cosine_fusion
  14.1 21.2 %all-gather.9.cloned.1.call-done = bf16[256,2048]{1,0:T(8,128)(2,1)} async-done(((bf16[128,2048]{1,0:T(8,128)(2,1)}), bf16[256,2048]{1,0:T(8,128)(2,1)}) %all-gather.9.cloned.1.call-update) | async-done | bytes 1048592 | tf_op jit(solution)/shard_map/all_gather | solution.py:103
  35.3 103.2 %all-gather.11.cloned.1.call-done = bf16[2048,3,1024]{2,0,1:T(8,128)(2,1)} async-done(((bf16[128,3,1024]{2,0,1:T(8,128)(2,1)}), bf16[2048,3,1024]{2,0,1:T(8,128)(2,1)}) %all-gather.11.cloned.1.call-update) | async-done | bytes 12582928 | tf_op jit(solution)/shard_map/all_gather | solution.py:96
  138.5 6.7 convolution_bitcast_fusion.3
  146.1 0.7 fusion.65
  146.8 0.8 subtract_convert_fusion.3
  147.7 0.9 fusion.67
  149.3 0.5 convolution_convert_fusion.2
  149.8 42.2 %all-gather.13.cloned.1.call-done = bf16[1024,2048]{1,0:T(8,128)(2,1)} async-done(((bf16[1024,128]{1,0:T(8,128)(2,1)}), bf16[1024,2048]{1,0:T(8,128)(2,1)}) %all-gather.13.cloned.1.call-update) | async-done | bytes 4194320 | tf_op jit(solution)/shard_map/all_gather | solution.py:97
  192.0 4.8 fusion.68
  196.9 30.2 %reduce-scatter.9.cloned.1.call-done = f32[128,2048]{1,0:T(8,128)} async-done(((f32[256,2048]{1,0:T(8,128)}), f32[128,2048]{1,0:T(8,128)}) %reduce-scatter.9.cloned.1.call-update) | async-done | bytes 1048592 | tf_op jit(solution)/shard_map/reduce_scatter | solution.py:126
  227.1 1.6 multiply_reduce_fusion.3
  228.7 0.9 multiply_convert_fusion.4
  229.7 3.1 copy.121
  232.9 0.7 all-gather.21.cloned.1.call-update
  233.6 2.3 convert_element_type.99
  236.1 14.9 all-gather.15.cloned.1.call-done
  251.1 120.7 %all-gather.17.cloned.1.call-done = bf16[2048,2,2816]{2,0,1:T(8,128)(2,1)} async-done(((bf16[128,2,2816]{2,0,1:T(8,128)(2,1)}), bf16[2048,2,2816]{2,0,1:T(8,128)(2,1)}) %all-gather.17.cloned.1.call-update) | async-done | bytes 23068688 | tf_op jit(solution)/shard_map/all_gather | solution.py:98
  371.8 12.7 convolution_bitcast_fusion
  384.4 10.2 all-gather.21.cloned.1.call-done
  394.6 99.7 %all-gather.19.cloned.1.call-done = bf16[2816,2048]{1,0:T(8,128)(2,1)} async-done(((bf16[2816,128]{1,0:T(8,128)(2,1)}), bf16[2816,2048]{1,0:T(8,128)(2,1)}) %all-gather.19.cloned.1.call-update) | async-done | bytes 11534352 | tf_op jit(solution)/shard_map/all_gather | solution.py:99
  494.3 12.4 fusion.19
  506.7 12.5 convolution_bitcast_fusion.2
  519.3 30.2 %reduce-scatter.13.cloned.1.call-done = f32[128,2048]{1,0:T(8,128)} async-done(((f32[256,2048]{1,0:T(8,128)}), f32[128,2048]{1,0:T(8,128)}) %reduce-scatter.13.cloned.1.call-update) | async-done | bytes 1048592 | tf_op jit(solution)/shard_map/reduce_scatter | solution.py:164
  549.4 1.7 multiply_reduce_fusion.1
  551.2 1.2 fusion.64
  552.6 21.1 %all-gather.23.cloned.1.call-done = bf16[256,2048]{1,0:T(8,128)(2,1)} async-done(((bf16[128,2048]{1,0:T(8,128)(2,1)}), bf16[256,2048]{1,0:T(8,128)(2,1)}) %all-gather.23.cloned.1.call-update) | async-done | bytes 1048592 | tf_op jit(solution)/shard_map/all_gather | solution.py:172
  573.8 4.6 convolution_convert_fusion.3
  578.4 2.0 copy.104
  580.4 3.0 fusion.49
  583.4 1.3 convolution_convert_fusion.1
  584.7 4.8 fusion.20
  589.5 4.6 fusion.23
  594.2 2.1 copy.84
  596.3 2.3 add_convert_fusion.1
  598.9 1.0 copy.75
  599.9 1.2 copy.82
  601.2 1.1 pad_maximum_fusion.9
  602.3 1.2 copy.79
  603.5 1.0 copy.83
  604.6 9.3 fusion.2
  613.9 0.3 reduce-scatter.11.cloned.1.call-start
  614.2 8.5 convolution_convert_fusion
  622.7 20.0 %fusion.6 = f32[2048,2,2816]{2,0,1:T(8,128)} fusion(bf16[1,256,2816]{2,1,0:T(8,128)(2,1)} %get-tuple-element.98, bf16[1,256,2816]{2,1,0:T(8,128)(2,1)} %get-tuple-element.97, bf16[256,2048]{1,0:T(8,128)(2,1)S(1)} %copy-done.4), kind=kOutput, calls=%fused_computation.23 | convolution fusion | flops 5911347200 | bytes 50069504 | tf_op jit(solution)/shard_map/td,ctf->dcf/dot_general | solution.py:159
  642.8 1.2 copy-done.21
  644.0 5.6 fusion.69
  649.7 1.1 copy-done.20
  650.9 9.5 fusion.70
  660.5 1.1 copy-done.3
  661.9 15.6 fusion.37
  677.6 1.1 copy-done
  678.7 1.6 fusion.33
  680.3 39.2 %all-reduce = (f32[2048]{0:T(1024)}, f32[2048]{0:T(1024)}) all-reduce(f32[2048]{0:T(1024)S(1)} %get-tuple-element.91, f32[2048]{0:T(1024)S(1)} %get-tuple-element.89), channel_id=1, replica_groups=mesh['dp'=16,'mp'=2] {'dp','mp'}, use_global_device_ids=true, to_apply=%region_19.20 | all-reduce | flops 4096 | bytes 32768 | tf_op jit(solution)/shard_map/psum | solution.py:228
  719.6 2.9 fusion.29
  722.5 372.0 %reduce-scatter.21.cloned.1.call-done = f32[128,2,2816]{2,0,1:T(8,128)} async-done(((f32[2048,2,2816]{2,0,1:T(8,128)}), f32[128,2,2816]{2,0,1:T(8,128)}) %reduce-scatter.21.cloned.1.call-update) | async-done | bytes 2883600 | tf_op jit(solution)/shard_map/reduce_scatter | solution.py:232
  1094.5 5.6 copy.87
  1100.2 101.7 %reduce-scatter.19.cloned.1.call-done = f32[1024,128]{1,0:T(8,128)} async-done(((f32[1024,2048]{1,0:T(8,128)}), f32[1024,128]{1,0:T(8,128)}) %reduce-scatter.19.cloned.1.call-update) | async-done | bytes 524304 | tf_op jit(solution)/shard_map/reduce_scatter | solution.py:231
  1201.9 231.4 %reduce-scatter.23.cloned.1.call-done = f32[2816,128]{1,0:T(8,128)} async-done(((f32[2816,2048]{1,0:T(8,128)}), f32[2816,128]{1,0:T(8,128)}) %reduce-scatter.23.cloned.1.call-update) | async-done | bytes 1441808 | tf_op jit(solution)/shard_map/reduce_scatter | solution.py:233
  1433.3 247.0 %reduce-scatter.17.cloned.1.call-done = f32[128,3,1024]{2,0,1:T(8,128)} async-done(((f32[2048,3,1024]{2,0,1:T(8,128)}), f32[128,3,1024]{2,0,1:T(8,128)}) %reduce-scatter.17.cloned.1.call-update) | async-done | bytes 1572880 | tf_op jit(solution)/shard_map/reduce_scatter | solution.py:230
  (112 shorter events, 4.0 us)
Async XLA Ops:
  7.2 4.0 copy-start.19
  7.2 28.1 %all-gather.9.cloned.1.call-start = ((), (), s32[]{:S(2)}) async-start(), calls=%async_computation.8 | async-start | bytes 1572864 | tf_op jit(solution)/shard_map/all_gather | solution.py:103
  8.6 0.5 copy-start.28
  11.1 1.2 copy-start.23
  11.1 2.0 copy-start.32
  11.1 127.4 %all-gather.11.cloned.1.call-start = ((), (), s32[]{:S(2)}) async-start(), calls=%async_computation.9 | async-start | bytes 13369344 | tf_op jit(solution)/shard_map/all_gather | solution.py:96
  12.2 179.8 %all-gather.13.cloned.1.call-start = ((), (), s32[]{:S(2)}) async-start(), calls=%async_computation.10 | async-start | bytes 4456448 | tf_op jit(solution)/shard_map/all_gather | solution.py:97
  13.0 214.0 %reduce-scatter.9.cloned.1.call-start = ((), (), s32[]{:S(2)}) async-start(), calls=%async_computation.11 | async-start | bytes 3145728 | tf_op jit(solution)/shard_map/reduce_scatter | solution.py:126
  145.9 3.4 copy-start.14
  147.6 0.9 copy-start.15
  147.6 1.0 copy-start.16
  147.7 1.1 copy-start.17
  147.7 1.3 copy-start.18
  149.8 47.0 %copy-start.22 = (bf16[8,128,256]{2,1,0:T(8,128)(2,1)}, bf16[8,128,256]{2,1,0:T(8,128)(2,1)S(1)}, u32[]{:S(2)}) copy-start(bf16[8,128,256]{2,1,0:T(8,128)(2,1)S(1)} %convolution_convert_fusion.2) | copy-start | bytes 1572868
  196.8 31.9 %copy-start.24 = (f32[2048]{0:T(1024)S(1)}, f32[2048]{0:T(1024)}, u32[]{:S(2)}) copy-start(f32[2048]{0:T(1024)} %param.13) | copy-start | bytes 24580
  196.8 54.3 %all-gather.15.cloned.1.call-start = ((), (), s32[]{:S(2)}) async-start(), calls=%async_computation.12 | async-start | bytes 1572864 | tf_op jit(solution)/shard_map/all_gather | solution.py:134
  228.7 322.5 %copy-start.26 = (f32[128]{0:T(128)}, f32[128]{0:T(128)S(1)}, u32[]{:S(2)}) copy-start(f32[128]{0:T(128)S(1)} %add_rsqrt_fusion) | copy-start | bytes 1540
  229.7 142.1 %all-gather.17.cloned.1.call-start = ((), (), s32[]{:S(2)}) async-start(), calls=%async_computation.13 | async-start | bytes 24510464 | tf_op jit(solution)/shard_map/all_gather | solution.py:98
  232.8 161.8 %all-gather.21.cloned.1.call-start = ((), (), s32[]{:S(2)}) async-start(), calls=%async_computation.16 | async-start | bytes 1572864 | tf_op jit(solution)/shard_map/all_gather | solution.py:153
  233.6 260.7 %all-gather.19.cloned.1.call-start = ((), (), s32[]{:S(2)}) async-start(), calls=%async_computation.14 | async-start | bytes 12255232 | tf_op jit(solution)/shard_map/all_gather | solution.py:99
  235.9 313.5 %reduce-scatter.13.cloned.1.call-start = ((), (), s32[]{:S(2)}) async-start(), calls=%async_computation.17 | async-start | bytes 3145728 | tf_op jit(solution)/shard_map/reduce_scatter | solution.py:164
  519.2 54.6 %all-gather.23.cloned.1.call-start = ((), (), s32[]{:S(2)}) async-start(), calls=%async_computation.18 | async-start | bytes 1572864 | tf_op jit(solution)/shard_map/all_gather | solution.py:172
  549.4 1.7 copy-start.1
  549.4 1.7 copy-start.6
  551.2 1.2 copy-start.30
  552.3 125.3 %reduce-scatter.15.cloned.1.call-start = ((), (), s32[]{:S(2)}) async-start(), calls=%async_computation.19 | async-start | bytes 1572864 | tf_op jit(solution)/shard_map/reduce_scatter | solution.py:218
  580.4 3.0 copy-start.5
  594.2 2.1 copy-start.8
  601.2 12.7 copy-start.12
  601.2 3.4 copy-start.10
  604.6 9.6 copy-start.9
  613.9 105.7 %reduce-scatter.11.cloned.1.call-start = ((), (), s32[]{:S(2)}) async-start(), calls=%async_computation.15 | async-start | bytes 1572864 | tf_op jit(solution)/shard_map/reduce_scatter | solution.py:140
  614.2 8.6 copy-start.4
  622.7 471.9 %reduce-scatter.21.cloned.1.call-start = ((), (), s32[]{:S(2)}) async-start(), calls=%async_computation.22 | async-start | bytes 49020928 | tf_op jit(solution)/shard_map/reduce_scatter | solution.py:232
  642.7 1.3 copy-start.21
  642.7 559.1 %reduce-scatter.19.cloned.1.call-start = ((), (), s32[]{:S(2)}) async-start(), calls=%async_computation.21 | async-start | bytes 8912896 | tf_op jit(solution)/shard_map/reduce_scatter | solution.py:231
  649.7 1.2 copy-start.20
  649.7 783.6 %reduce-scatter.23.cloned.1.call-start = ((), (), s32[]{:S(2)}) async-start(), calls=%async_computation.23 | async-start | bytes 24510464 | tf_op jit(solution)/shard_map/reduce_scatter | solution.py:233
  660.4 1.2 copy-start.3
  660.4 1.4 copy-start.11
  660.4 1.5 copy-start.13
  660.4 1019.9 %reduce-scatter.17.cloned.1.call-start = ((), (), s32[]{:S(2)}) async-start(), calls=%async_computation.20 | async-start | bytes 26738688 | tf_op jit(solution)/shard_map/reduce_scatter | solution.py:230
  677.5 1.2 copy-start
  677.5 1.2 copy-start.25
  677.5 1.2 copy-start.29
  677.5 42.0 %copy-start.2 = (f32[128,2048]{1,0:T(8,128)S(1)}, f32[128,2048]{1,0:T(8,128)}, u32[]{:S(2)}) copy-start(f32[128,2048]{1,0:T(8,128)} %reduce-scatter.13.cloned.1.call-done) | copy-start | bytes 3145732
  677.5 42.0 %copy-start.7 = (bf16[128,2048]{1,0:T(8,128)(2,1)S(1)}, bf16[128,2048]{1,0:T(8,128)(2,1)}, u32[]{:S(2)}) copy-start(bf16[128,2048]{1,0:T(8,128)(2,1)} %param.11) | copy-start | bytes 1572868
  677.5 42.0 %copy-start.27 = (f32[128]{0:T(128)S(1)}, f32[128]{0:T(128)}, u32[]{:S(2)}) copy-start(f32[128]{0:T(128)} %copy-done.26) | copy-start | bytes 1540
  677.5 42.0 %copy-start.31 = (f32[128]{0:T(128)S(1)}, f32[128]{0:T(128)}, u32[]{:S(2)}) copy-start(f32[128]{0:T(128)} %copy-done.30) | copy-start | bytes 1540
Sparse Core Ops, SparseCore 0:
  11.3 23.9 all-gather.8
  38.1 100.4 all-gather.10
  141.3 50.7 all-gather.12
  197.0 30.0 reduce-scatter.8
  229.8 21.2 all-gather.14
  253.1 118.6 all-gather.16
  373.3 21.2 all-gather.20
  397.3 96.9 all-gather.18
  519.3 30.0 reduce-scatter.12
  552.5 21.2 all-gather.22
  614.0 20.3 reduce-scatter.14
  637.1 20.3 reduce-scatter.10
  661.7 432.7 reduce-scatter.20
  1099.0 102.7 reduce-scatter.18
  1206.4 226.8 reduce-scatter.22
  1437.8 242.4 reduce-scatter.16
where the time goes:
time: 1690 us
  waiting for transfers between devices  1450 us (86%)
  matrix products  137 us (8%)
  blocking collectives  39.2 us (2%)
  local copies, waits for them, and re-layouts  24.8 us (1%)
  other arithmetic  23.1 us (1%)
    reduce_scatter x1, waiting for transfers between devices, on_device(): lax.psum_scatter(mlp_sums[0], 'dp', scatter_dimension=0, tiled=True)  372 us
    reduce_scatter x1, waiting for transfers between devices, on_device(): lax.psum_scatter(grad_qkv, 'dp', scatter_dimension=0, tiled=True)  247 us
    reduce_scatter x1, waiting for transfers between devices, on_device(): lax.psum_scatter(mlp_sums[1], 'dp', scatter_dimension=1, tiled=True)  231 us
    all_gather x1, waiting for transfers between devices, on_device(): lax.all_gather(masters[2], 'dp', axis=0, tiled=True)  121 us
    all_gather x1, waiting for transfers between devices, on_device(): lax.all_gather(masters[0], 'dp', axis=0, tiled=True)  103 us
    reduce_scatter x1, waiting for transfers between devices, on_device(): lax.psum_scatter(grad_out, 'dp', scatter_dimension=1, tiled=True)  102 us
    all_gather x1, waiting for transfers between devices, on_device(): lax.all_gather(masters[3], 'dp', axis=1, tiled=True)  99.7 us
    all_gather x1, waiting for transfers between devices, on_device(): lax.all_gather(masters[1], 'dp', axis=1, tiled=True)  42.2 us
  transfers between devices with their start and end apart: 16, of which 14 were waited for; matrix products, arithmetic and copies ran while one was open for 6% of the time, Pallas kernels for 0%

commit v1 on v0

--- a/solution.py
+++ b/solution.py
@@ -75,6 +75,13 @@
     )
     allowed = (seg_rows[:, None] == segment[None, :]) & (places[None, :] <= place_rows[:, None])
     return jnp.where(allowed[None], raw_scores * scale, MASKED)
+
+
+def scatter_sum(gradient, dimension):
+    total = lax.psum_scatter(
+        gradient.astype(jnp.bfloat16), "dp", scatter_dimension=dimension, tiled=True
+    )
+    return total.astype(jnp.float32)
 
 
 def on_device(tokens, doc_lengths, cotangent, gain_attn, gain_mlp, w_qkv, w_out, w_gate_up, w_down):
@@ -227,10 +234,10 @@
     input_grad = d_resid_mid + d_resid_first
     gain_totals = lax.psum((gain_attn_part, gain_mlp_part), ("dp", "mp"))
     weight_sums = (
-        lax.psum_scatter(grad_qkv, "dp", scatter_dimension=0, tiled=True),
-        lax.psum_scatter(grad_out, "dp", scatter_dimension=1, tiled=True),
-        lax.psum_scatter(mlp_sums[0], "dp", scatter_dimension=0, tiled=True),
-        lax.psum_scatter(mlp_sums[1], "dp", scatter_dimension=1, tiled=True),
+        scatter_sum(grad_qkv, 0),
+        scatter_sum(grad_out, 1),
+        scatter_sum(mlp_sums[0], 0),
+        scatter_sum(mlp_sums[1], 1),
     )
     return (
         block_out,

time: 1690 us -> 1250 us (0.74)
  waiting for transfers between devices: 1450 us -> 994 us
  local copies, waits for them, and re-layouts: 24.8 us -> 46.6 us
  matrix products: 137 us -> 118 us
    reduce_scatter x4 -> x2, waiting for transfers between devices: 952 us -> 364 us  [scatter_sum(): lax.psum_scatter(gradient.astype(jnp.bfloat16), 'dp', scatter_dimension=d...]
    unnamed x16 -> x18, waiting for transfers between devices: 0.94 us -> 137 us
    unnamed x73 -> x79, local copies, waits for them, and re-layouts: 15.4 us -> 40.1 us
  transfers between devices with their start and end apart: 16 -> 16, of which waited for: 14 -> 14; matrix products, arithmetic and copies ran while one was open for 6% -> 8% of each run, Pallas kernels for 0% -> 0%
where the time goes in v1:
time: 1250 us; the launch traced here: 1240 us
  waiting for transfers between devices  994 us (80%)
  matrix products  118 us (9%)
  local copies, waits for them, and re-layouts  46.6 us (4%)
  blocking collectives  41 us (3%)
  other arithmetic  26.6 us (2%)
  between operations  14.9 us (1%)
    reduce_scatter x2, waiting for transfers between devices, scatter_sum(): lax.psum_scatter(gradient.astype(jnp.bfloat16), 'dp', scatter_dimension=d...  364 us
    unnamed x18, waiting for transfers between devices  137 us
    all_gather x1, waiting for transfers between devices, on_device(): lax.all_gather(masters[2], 'dp', axis=0, tiled=True)  121 us
    all_gather x1, waiting for transfers between devices, on_device(): lax.all_gather(masters[0], 'dp', axis=0, tiled=True)  103 us
    all_gather x1, waiting for transfers between devices, on_device(): lax.all_gather(masters[3], 'dp', axis=1, tiled=True)  99.7 us
    all_gather x1, waiting for transfers between devices, on_device(): lax.all_gather(masters[1], 'dp', axis=1, tiled=True)  42.2 us
    psum x1, blocking collectives, on_device(): gain_totals = lax.psum((gain_attn_part, gain_mlp_part), ('dp', 'mp'))  41 us
    unnamed x79, local copies, waits for them, and re-layouts  40.1 us
  transfers between devices with their start and end apart: 16, of which 14 were waited for; matrix products, arithmetic and copies ran while one was open for 8% of the time, Pallas kernels for 0%

profile of v1, /device:TPU:0, one launch (start us, length us, event | category | flops | bytes accessed | tf_op | source)
XLA Modules:
  0.0 1241.9 jit_solution(8914130683031569904)
XLA Ops:
  7.2 1.3 fusion.33
  9.1 2.0 fusion.30
  11.2 1.0 convert_element_type.112
  12.3 0.7 convert_element_type.119
  14.1 21.2 %all-gather.9.cloned.1.call-done = bf16[256,2048]{1,0:T(8,128)(2,1)} async-done(((bf16[128,2048]{1,0:T(8,128)(2,1)}), bf16[256,2048]{1,0:T(8,128)(2,1)}) %all-gather.9.cloned.1.call-update) | async-done | bytes 1048592 | tf_op jit(solution)/shard_map/all_gather | solution.py:110
  35.3 103.2 %all-gather.11.cloned.1.call-done = bf16[2048,3,1024]{2,0,1:T(8,128)(2,1)} async-done(((bf16[128,3,1024]{2,0,1:T(8,128)(2,1)}), bf16[2048,3,1024]{2,0,1:T(8,128)(2,1)}) %all-gather.11.cloned.1.call-update) | async-done | bytes 12582928 | tf_op jit(solution)/shard_map/all_gather | solution.py:103
  138.5 6.7 convolution_bitcast_fusion.3
  146.1 0.7 fusion.63
  146.8 0.8 subtract_convert_fusion.3
  147.7 0.9 fusion.65
  149.8 42.2 %all-gather.13.cloned.1.call-done = bf16[1024,2048]{1,0:T(8,128)(2,1)} async-done(((bf16[1024,128]{1,0:T(8,128)(2,1)}), bf16[1024,2048]{1,0:T(8,128)(2,1)}) %all-gather.13.cloned.1.call-update) | async-done | bytes 4194320 | tf_op jit(solution)/shard_map/all_gather | solution.py:104
  192.0 4.8 fusion.66
  196.9 30.2 %reduce-scatter.13.cloned.1.call-done = f32[128,2048]{1,0:T(8,128)} async-done(((f32[256,2048]{1,0:T(8,128)}), f32[128,2048]{1,0:T(8,128)}) %reduce-scatter.13.cloned.1.call-update) | async-done | bytes 1048592 | tf_op jit(solution)/shard_map/reduce_scatter | solution.py:133
  227.1 1.6 multiply_reduce_fusion.3
  228.7 0.9 multiply_convert_fusion.4
  229.7 3.1 copy.150
  232.9 0.7 all-gather.21.cloned.1.call-update
  233.6 2.3 convert_element_type.123
  236.1 14.9 %all-gather.15.cloned.1.call-done = bf16[256,2048]{1,0:T(8,128)(2,1)} async-done(((bf16[128,2048]{1,0:T(8,128)(2,1)}), bf16[256,2048]{1,0:T(8,128)(2,1)}) %all-gather.15.cloned.1.call-update) | async-done | bytes 1048592 | tf_op jit(solution)/shard_map/all_gather | solution.py:141
  251.1 120.7 %all-gather.17.cloned.1.call-done = bf16[2048,2,2816]{2,0,1:T(8,128)(2,1)} async-done(((bf16[128,2,2816]{2,0,1:T(8,128)(2,1)}), bf16[2048,2,2816]{2,0,1:T(8,128)(2,1)}) %all-gather.17.cloned.1.call-update) | async-done | bytes 23068688 | tf_op jit(solution)/shard_map/all_gather | solution.py:105
  371.8 12.7 %convolution_bitcast_fusion = f32[2,256,2816]{2,1,0:T(8,128)} fusion(bf16[2048,2,2816]{2,0,1:T(8,128)(2,1)} %all-gather.17.cloned.1.call-done, bf16[256,2048]{1,0:T(8,128)(2,1)} %all-gather.15.cloned.1.call-done), kind=kOutput, calls=%fused_computation.4 | convolution fusion | flops 5905580032 | bytes 29884416 | tf_op jit(solution)/shard_map/td,dcf->ctf/dot_general | solution.py:142
  384.4 10.2 all-gather.21.cloned.1.call-done
  394.6 99.7 %all-gather.19.cloned.1.call-done = bf16[2816,2048]{1,0:T(8,128)(2,1)} async-done(((bf16[2816,128]{1,0:T(8,128)(2,1)}), bf16[2816,2048]{1,0:T(8,128)(2,1)}) %all-gather.19.cloned.1.call-update) | async-done | bytes 11534352 | tf_op jit(solution)/shard_map/all_gather | solution.py:106
  494.3 12.4 fusion.18
  506.7 12.5 %convolution_bitcast_fusion.2 = f32[256,2048]{1,0:T(8,128)} fusion(bf16[2048,2,2816]{2,0,1:T(8,128)(2,1)} %all-gather.17.cloned.1.call-done, bf16[1,256,2816]{2,1,0:T(8,128)(2,1)} %get-tuple-element.106, bf16[1,256,2816]{2,1,0:T(8,128)(2,1)} %get-tuple-element.105), kind=kOutput, calls=%fused_computation.16 | convolution fusion | flops 5907021824 | bytes 28049408 | tf_op jit(solution)/shard_map/ctf,dcf->td/dot_general | solution.py:172
  519.3 30.2 %reduce-scatter.17.cloned.1.call-done = f32[128,2048]{1,0:T(8,128)} async-done(((f32[256,2048]{1,0:T(8,128)}), f32[128,2048]{1,0:T(8,128)}) %reduce-scatter.17.cloned.1.call-update) | async-done | bytes 1048592 | tf_op jit(solution)/shard_map/reduce_scatter | solution.py:171
  549.5 1.7 multiply_reduce_fusion.1
  551.2 1.2 fusion.62
  552.7 21.1 %all-gather.23.cloned.1.call-done = bf16[256,2048]{1,0:T(8,128)(2,1)} async-done(((bf16[128,2048]{1,0:T(8,128)(2,1)}), bf16[256,2048]{1,0:T(8,128)(2,1)}) %all-gather.23.cloned.1.call-update) | async-done | bytes 1048592 | tf_op jit(solution)/shard_map/all_gather | solution.py:179
  573.8 4.6 convolution_convert_fusion.7
  578.4 2.0 copy.133
  580.4 3.0 fusion.47
  583.4 1.3 convolution_convert_fusion.5
  584.7 4.8 fusion.19
  589.6 4.7 fusion.22
  594.3 2.1 copy.109
  596.4 2.3 add_convert_fusion.1
  599.2 1.0 copy.107
  601.6 9.4 fusion.2
  611.3 8.4 convolution_convert_fusion.4
  619.8 4.4 convolution_convert_fusion.3
  624.3 6.4 copy.125
  630.8 1.2 copy-done.19
  631.9 6.0 convolution_convert_fusion.1
  637.9 15.8 %copy.127 = bf16[2816,2048]{0,1:T(8,128)(2,1)} copy(bf16[2816,2048]{1,0:T(8,128)(2,1)} %convolution_convert_fusion.1) | data formatting | bytes 23068672
  653.8 1.2 copy-done.8
  655.3 7.4 convolution_convert_fusion.2
  662.8 1.2 copy-done.3
  663.9 0.6 copy-done.16
  664.5 13.2 %convolution_convert_fusion = bf16[2048,2,2816]{2,0,1:T(8,128)(2,1)} fusion(bf16[1,256,2816]{2,1,0:T(8,128)(2,1)} %get-tuple-element.106, bf16[1,256,2816]{2,1,0:T(8,128)(2,1)S(1)} %copy-done.16, bf16[256,2048]{1,0:T(8,128)(2,1)S(1)} %copy-done.3), kind=kOutput, calls=%fused_computation.1 | convolution fusion | flops 5922881536 | bytes 27000832 | tf_op jit(solution)/shard_map/td,ctf->dcf/dot_general | solution.py:166
  677.8 1.0 copy-done
  678.8 1.5 fusion.32
  680.3 41.0 %all-reduce = (f32[2048]{0:T(1024)}, f32[2048]{0:T(1024)}) all-reduce(f32[2048]{0:T(1024)S(1)} %get-tuple-element.99, f32[2048]{0:T(1024)S(1)} %get-tuple-element.97), channel_id=1, replica_groups=mesh['dp'=16,'mp'=2] {'dp','mp'}, use_global_device_ids=true, to_apply=%region_19.20 | all-reduce | flops 4096 | bytes 32768 | tf_op jit(solution)/shard_map/psum | solution.py:235
  721.3 2.9 fusion.28
  724.1 7.5 reduce-scatter.25.cloned.1.call-done
  731.7 1.1 copy.126
  732.8 0.8 convert_element_type.137
  733.6 128.1 %reduce-scatter.27.cloned.1.call-done = bf16[128,2816]{1,0:T(8,128)(2,1)} async-done(((bf16[2048,2816]{1,0:T(8,128)(2,1)}), bf16[128,2816]{1,0:T(8,128)(2,1)}) %reduce-scatter.27.cloned.1.call-update) | async-done | bytes 720912
  861.7 1.5 copy.128
  863.2 1.2 convert_element_type.141
  864.4 135.5 %reduce-scatter.21.cloned.1.call-done = bf16[128,3,1024]{2,0,1:T(8,128)(2,1)} async-done(((bf16[2048,3,1024]{2,0,1:T(8,128)(2,1)}), bf16[128,3,1024]{2,0,1:T(8,128)(2,1)}) %reduce-scatter.21.cloned.1.call-update) | async-done | bytes 786448 | tf_op jit(solution)/shard_map/reduce_scatter | solution.py:81
  999.8 2.5 convert_element_type.135
  1002.3 228.2 %reduce-scatter.23.cloned.1.call-done = bf16[128,2,2816]{2,0,1:T(8,128)(2,1)} async-done(((bf16[2048,2,2816]{2,0,1:T(8,128)(2,1)}), bf16[128,2,2816]{2,0,1:T(8,128)(2,1)}) %reduce-scatter.23.cloned.1.call-update) | async-done | bytes 1441808 | tf_op jit(solution)/shard_map/reduce_scatter | solution.py:81
  1230.5 4.4 copy.112
  (121 shorter events, 7.4 us)
Async XLA Ops:
  7.2 4.0 copy-start.15
  7.2 28.1 %all-gather.9.cloned.1.call-start = ((), (), s32[]{:S(2)}) async-start(), calls=%async_computation.8 | async-start | bytes 1572864 | tf_op jit(solution)/shard_map/all_gather | solution.py:110
  8.6 0.5 copy-start.29
  11.1 1.2 copy-start.20
  11.1 2.0 copy-start.33
  11.1 127.4 %all-gather.11.cloned.1.call-start = ((), (), s32[]{:S(2)}) async-start(), calls=%async_computation.9 | async-start | bytes 13369344 | tf_op jit(solution)/shard_map/all_gather | solution.py:103
  12.2 179.8 %all-gather.13.cloned.1.call-start = ((), (), s32[]{:S(2)}) async-start(), calls=%async_computation.10 | async-start | bytes 4456448 | tf_op jit(solution)/shard_map/all_gather | solution.py:104
  13.0 214.0 %reduce-scatter.13.cloned.1.call-start = ((), (), s32[]{:S(2)}) async-start(), calls=%async_computation.11 | async-start | bytes 3145728 | tf_op jit(solution)/shard_map/reduce_scatter | solution.py:133
  145.9 3.4 copy-start.10
  147.6 0.9 copy-start.11
  147.6 1.0 copy-start.12
  147.7 1.2 copy-start.13
  147.7 1.3 copy-start.14
  149.8 47.0 %copy-start.17 = (bf16[8,128,256]{2,1,0:T(8,128)(2,1)}, bf16[8,128,256]{2,1,0:T(8,128)(2,1)S(1)}, u32[]{:S(2)}) copy-start(bf16[8,128,256]{2,1,0:T(8,128)(2,1)S(1)} %convolution_convert_fusion.6) | copy-start | bytes 1572868
  196.8 31.9 %copy-start.25 = (f32[2048]{0:T(1024)S(1)}, f32[2048]{0:T(1024)}, u32[]{:S(2)}) copy-start(f32[2048]{0:T(1024)} %param.13) | copy-start | bytes 24580
  196.8 54.3 %all-gather.15.cloned.1.call-start = ((), (), s32[]{:S(2)}) async-start(), calls=%async_computation.12 | async-start | bytes 1572864 | tf_op jit(solution)/shard_map/all_gather | solution.py:141
  228.7 322.5 %copy-start.27 = (f32[128]{0:T(128)}, f32[128]{0:T(128)S(1)}, u32[]{:S(2)}) copy-start(f32[128]{0:T(128)S(1)} %add_rsqrt_fusion) | copy-start | bytes 1540
  229.7 142.1 %all-gather.17.cloned.1.call-start = ((), (), s32[]{:S(2)}) async-start(), calls=%async_computation.13 | async-start | bytes 24510464 | tf_op jit(solution)/shard_map/all_gather | solution.py:105
  232.8 161.8 %all-gather.21.cloned.1.call-start = ((), (), s32[]{:S(2)}) async-start(), calls=%async_computation.16 | async-start | bytes 1572864 | tf_op jit(solution)/shard_map/all_gather | solution.py:160
  233.6 260.7 %all-gather.19.cloned.1.call-start = ((), (), s32[]{:S(2)}) async-start(), calls=%async_computation.14 | async-start | bytes 12255232 | tf_op jit(solution)/shard_map/all_gather | solution.py:106
  235.9 313.6 %reduce-scatter.17.cloned.1.call-start = ((), (), s32[]{:S(2)}) async-start(), calls=%async_computation.17 | async-start | bytes 3145728 | tf_op jit(solution)/shard_map/reduce_scatter | solution.py:171
  519.2 54.6 %all-gather.23.cloned.1.call-start = ((), (), s32[]{:S(2)}) async-start(), calls=%async_computation.18 | async-start | bytes 1572864 | tf_op jit(solution)/shard_map/all_gather | solution.py:179
  549.5 1.7 copy-start.1
  549.5 1.7 copy-start.5
  551.2 1.2 copy-start.31
  552.4 125.4 %reduce-scatter.19.cloned.1.call-start = ((), (), s32[]{:S(2)}) async-start(), calls=%async_computation.19 | async-start | bytes 1572864 | tf_op jit(solution)/shard_map/reduce_scatter | solution.py:225
  580.4 3.0 copy-start.4
  594.3 2.1 copy-start.7
  600.5 1.0 copy-start.22
  601.6 9.4 copy-start.24
  601.6 9.7 copy-start.9
  611.0 110.2 %reduce-scatter.15.cloned.1.call-start = ((), (), s32[]{:S(2)}) async-start(), calls=%async_computation.15 | async-start | bytes 1572864 | tf_op jit(solution)/shard_map/reduce_scatter | solution.py:147
  611.3 8.5 copy-start.18
  619.8 111.9 %reduce-scatter.25.cloned.1.call-start = ((), (), s32[]{:S(2)}) async-start(), calls=%async_computation.22 | async-start | bytes 4456448
  630.7 1.2 copy-start.19
  630.7 231.0 %reduce-scatter.27.cloned.1.call-start = ((), (), s32[]{:S(2)}) async-start(), calls=%async_computation.23 | async-start | bytes 12255232
  653.7 1.2 copy-start.8
  653.7 1.4 copy-start.21
  653.7 1.6 copy-start.23
  653.8 346.0 %reduce-scatter.21.cloned.1.call-start = ((), (), s32[]{:S(2)}) async-start(), calls=%async_computation.20 | async-start | bytes 13369344 | tf_op jit(solution)/shard_map/reduce_scatter | solution.py:81
  662.7 1.2 copy-start.3
  662.7 1.8 copy-start.16
  662.7 567.8 %reduce-scatter.23.cloned.1.call-start = ((), (), s32[]{:S(2)}) async-start(), calls=%async_computation.21 | async-start | bytes 24510464 | tf_op jit(solution)/shard_map/reduce_scatter | solution.py:81
  677.7 1.1 copy-start
  677.7 1.1 copy-start.26
  677.7 1.1 copy-start.30
  677.7 43.5 %copy-start.2 = (f32[128,2048]{1,0:T(8,128)S(1)}, f32[128,2048]{1,0:T(8,128)}, u32[]{:S(2)}) copy-start(f32[128,2048]{1,0:T(8,128)} %reduce-scatter.17.cloned.1.call-done) | copy-start | bytes 3145732
  677.7 43.5 %copy-start.6 = (bf16[128,2048]{1,0:T(8,128)(2,1)S(1)}, bf16[128,2048]{1,0:T(8,128)(2,1)}, u32[]{:S(2)}) copy-start(bf16[128,2048]{1,0:T(8,128)(2,1)} %param.11) | copy-start | bytes 1572868
  677.7 43.5 %copy-start.28 = (f32[128]{0:T(128)S(1)}, f32[128]{0:T(128)}, u32[]{:S(2)}) copy-start(f32[128]{0:T(128)} %copy-done.27) | copy-start | bytes 1540
  677.7 43.5 %copy-start.32 = (f32[128]{0:T(128)S(1)}, f32[128]{0:T(128)}, u32[]{:S(2)}) copy-start(f32[128]{0:T(128)} %copy-done.31) | copy-start | bytes 1540
Sparse Core Ops, SparseCore 0:
  11.3 23.9 all-gather.8
  38.1 100.4 all-gather.10
  141.3 50.7 all-gather.12
  197.0 30.0 reduce-scatter.12
  229.8 21.2 all-gather.14
  253.1 118.6 all-gather.16
  373.3 21.2 all-gather.20
  397.3 96.9 all-gather.18
  519.4 30.0 reduce-scatter.16
  552.5 21.2 all-gather.22
  611.1 20.3 reduce-scatter.18
  634.2 20.3 reduce-scatter.14
  658.5 73.1 reduce-scatter.24
  735.6 126.0 reduce-scatter.26
  865.6 134.1 reduce-scatter.20
  1003.8 226.6 reduce-scatter.22
